TPU v7x, 128 devices: a whole 4x4x4 slice. The times are simulated.
128 devices in a mesh: ctx: 16 (over x, y), fsdp: 8 (over z, core).
Axes of the slice: x: 4, y: 4, z: 4, core: 2. Of those that a mesh axis runs over, the one named last changes fastest.
Arguments:
- tokens: bfloat16 [16384, 4096], P(('ctx', 'fsdp')), may hold values from -360 to 360
- norm_gain: float32 [4096], replicated, may hold values from 0.1 to 1.9
- qkv_weight: bfloat16 [3, 4096, 2048], P(None, 'ctx', 'fsdp'), may hold values from -1 to 1
- out_weight: bfloat16 [2048, 4096], P('fsdp', 'ctx'), may hold values from -1 to 1
- layout: int32 [128, 16], replicated, may hold values from 0 to 127, as said below
Outputs:
- branch_out: bfloat16 [16384, 4096], P(('ctx', 'fsdp'))
Inputs may be any that keep to these rules, and one draw needn't show every extreme that they name: `layout`: every entry of query block i names a block of 0 to i. With the blocks taken in spans of 8, the query blocks of one span name at most 2 distinct blocks of any other span, and some pair of spans reaches 2 in every draw.
All inputs are finite; a program needn't handle non-finite values.
Results may differ from a plain program's by a relative error of at most 0.015.
Values may be sent and summed in bfloat16 or wider, within the bound.
A program may use at most 128 MiB of HBM per device.

v0:
```python
import math
import jax
import jax.numpy as jnp
from jax import lax
from jax.sharding import PartitionSpec as P

HEAD_DIM = 128
BLK = 128
SUMMARY = 16
EPSILON = 1e-05


def normalize(tokens, norm_gain):
    features = tokens.astype(jnp.float32)
    mean_square = jnp.mean(features * features, axis=-1, keepdims=True)
    return (features * lax.rsqrt(mean_square + EPSILON) * norm_gain).astype(jnp.bfloat16)


def shards(tokens, norm_gain, qkv_weight, out_weight, layout):
    normed = normalize(tokens, norm_gain)
    gathered = lax.all_gather(normed, "fsdp", axis=0, tiled=True)
    span_rows = gathered.shape[0]
    local_width = qkv_weight.shape[2]
    heads_here = local_width // HEAD_DIM
    projected = jnp.einsum(
        "td,cdi->cti",
        gathered,
        lax.all_gather(qkv_weight, "ctx", axis=1, tiled=True),
        preferred_element_type=jnp.float32,
    ).astype(jnp.bfloat16)
    queries, key_rows, value_rows = (projected[0], projected[1], projected[2])
    ctx_index = lax.axis_index("ctx")
    span_blocks = span_rows // BLK
    key_slots = 2 + SUMMARY
    first_block = ctx_index * span_blocks
    own_blocks = first_block + jnp.arange(span_blocks, dtype=jnp.int32)
    listed = lax.dynamic_slice_in_dim(layout, first_block, span_blocks, 0)
    key_index = jnp.concatenate([own_blocks[:, None], own_blocks[:, None] - 1, listed], axis=1)
    every_key, every_value = (
        lax.all_gather(key_rows, "ctx", axis=0, tiled=True),
        lax.all_gather(value_rows, "ctx", axis=0, tiled=True),
    )
    total_blocks = every_key.shape[0] // BLK
    pool_keys = every_key.reshape(total_blocks, BLK, local_width)
    pool_values = every_value.reshape(total_blocks, BLK, local_width)
    gather_index = jnp.maximum(key_index, 0)
    group_size = math.gcd(span_blocks, max(1, 512 // BLK))
    group_count = span_blocks // group_size
    score_scale = HEAD_DIM ** (-0.5)
    offsets = jnp.arange(BLK, dtype=jnp.int32)

    def attend(packed):
        group_queries, group_index, group_slots, group_blocks = packed
        key_blocks = pool_keys[group_index].reshape(
            group_size, key_slots, BLK, heads_here, HEAD_DIM
        )
        value_blocks = pool_values[group_index].reshape(
            group_size, key_slots, BLK, heads_here, HEAD_DIM
        )
        scores = (
            jnp.einsum(
                "bqhd,bnkhd->bhqnk", group_queries, key_blocks, preferred_element_type=jnp.float32
            )
            * score_scale
        )
        query_pos = group_blocks[:, None] * BLK + offsets[None, :]
        key_pos = group_slots[:, :, None] * BLK + offsets[None, None, :]
        allowed = (key_pos[:, None, :, :] <= query_pos[:, :, None, None]) & (
            key_pos[:, None, :, :] >= 0
        )
        allowed = allowed[:, None]
        scores = jnp.where(allowed, scores, -1e30)
        row_max = jnp.max(scores, axis=(3, 4), keepdims=True)
        weights = jnp.where(allowed, jnp.exp(scores - row_max), 0.0)
        denominator = jnp.sum(weights, axis=(3, 4), keepdims=True)
        weights = (weights / denominator).astype(jnp.bfloat16)
        blended = jnp.einsum(
            "bhqnk,bnkhd->bqhd", weights, value_blocks, preferred_element_type=jnp.float32
        )
        return blended.astype(jnp.bfloat16)

    packed_inputs = (
        queries.reshape(group_count, group_size, BLK, heads_here, HEAD_DIM),
        gather_index.reshape(group_count, group_size, key_slots),
        key_index.reshape(group_count, group_size, key_slots),
        own_blocks.reshape(group_count, group_size),
    )
    blended_all = lax.map(attend, packed_inputs)
    attended = blended_all.reshape(span_rows, local_width)
    projection = lax.all_gather(out_weight, "ctx", axis=1, tiled=True)
    return lax.psum_scatter(
        jnp.dot(attended, projection, preferred_element_type=jnp.float32).astype(jnp.bfloat16),
        "fsdp",
        scatter_dimension=0,
        tiled=True,
    )


def solution(mesh):
    placed = (P(("ctx", "fsdp"), None), P(), P(None, "ctx", "fsdp"), P("fsdp", "ctx"), P())
    return jax.shard_map(
        shards, mesh=mesh, in_specs=placed, out_specs=P(("ctx", "fsdp"), None), check_vma=False
    )
```

profile of v0, /device:TPU:1, one launch (start us, length us, event | category | flops | bytes accessed | tf_op | source)
XLA Modules:
  0.0 463.3 jit_solution(6775085235407852516)
XLA Ops:
  8.8 2.5 fusion.26
  11.4 62.3 %all-gather.10.cloned.1.call-done = bf16[3,4096,256]{2,1,0:T(8,128)(2,1)} async-done(((bf16[3,256,256]{2,1,0:T(8,128)(2,1)}), bf16[3,4096,256]{2,1,0:T(8,128)(2,1)}) %all-gather.10.cloned.1.call-update) | async-done | bytes 6291472 | tf_op jit(solution)/shard_map/all_gather | solution.py:28
  73.7 51.9 %all-gather.8.cloned.1.call-done = bf16[1024,4096]{1,0:T(8,128)(2,1)} async-done(((bf16[128,4096]{1,0:T(8,128)(2,1)}), bf16[1024,4096]{1,0:T(8,128)(2,1)}) %all-gather.8.cloned.1.call-update) | async-done | bytes 8388624 | tf_op jit(solution)/shard_map/all_gather | solution.py:21
  125.6 10.9 %fusion.30 = bf16[3,1024,256]{2,1,0:T(8,128)(2,1)S(1)} fusion(bf16[3,4096,256]{2,1,0:T(8,128)(2,1)} %all-gather.10.cloned.1.call-done, bf16[1024,4096]{1,0:T(8,128)(2,1)} %all-gather.8.cloned.1.call-done), kind=kOutput, calls=%fused_computation.40 | convolution fusion | flops 6443237376 | bytes 16252928 | tf_op jit(solution)/shard_map/td,cdi->cti/dot_general | solution.py:25
  139.3 68.6 %all-gather.14.cloned.1.call-done = bf16[1,16384,256]{2,1,0:T(8,128)(2,1)} async-done(((bf16[1,1024,256]{2,1,0:T(8,128)(2,1)}), bf16[1,16384,256]{2,1,0:T(8,128)(2,1)}) %all-gather.14.cloned.1.call-update) | async-done | bytes 8388624 | tf_op jit(solution)/shard_map/all_gather | solution.py:41
  207.9 72.4 %all-gather.16.cloned.1.call-done = bf16[1,16384,256]{2,1,0:T(8,128)(2,1)} async-done(((bf16[1,1024,256]{2,1,0:T(8,128)(2,1)}), bf16[1,16384,256]{2,1,0:T(8,128)(2,1)}) %all-gather.16.cloned.1.call-update) | async-done | bytes 8388624 | tf_op jit(solution)/shard_map/all_gather | solution.py:40
  280.3 116.7 %while.12 = (s32[]{:T(128)}, bf16[2,4,128,2,128]{4,3,2,1,0:T(2,128)(2,1)S(1)}, s32[2,4,18]{2,1,0:T(4,128)S(1)}, bf16[128,128,256]{2,1,0:T(8,128)(2,1)}, s32[2,4,...) while((s32[]{:T(128)}, ...), condition=%wide.region_4.5_spmd.clone.clone, body=%wide.region_1.4_spmd.clone.clone.sunk | while | flops 1243507456 | bytes 139060496 | solution.py:88
  280.6 3.5 compare_and_fusion.2
  284.2 8.9 %gather_fusion = bf16[72,128,256]{2,1,0:T(8,128)(2,1)} fusion(bf16[128,128,256]{2,1,0:T(8,128)(2,1)} %get-tuple-element.209, s32[1024]{0:T(1024)S(1)} %pad_clamp_fusion.2), kind=kCustom, calls=%fused_computation.1.clone.clone.1 | custom fusion | bytes 9437472 | tf_op jit(solution)/shard_map/while/body/eval_jaxpr/gather | solution.py:54
  293.1 7.7 %reshape.196 = bf16[4,18,128,2,128]{4,3,2,1,0:T(2,128)(2,1)} reshape(bf16[72,128,256]{2,1,0:T(8,128)(2,1)} %gather_fusion) | data formatting | bytes 9437184 | tf_op jit(solution)/shard_map/while/body/eval_jaxpr/reshape | solution.py:54
  300.8 3.6 copy.44
  309.7 2.5 fusion.51
  312.2 9.0 %gather_fusion.1 = bf16[72,128,256]{2,1,0:T(8,128)(2,1)} fusion(bf16[128,128,256]{2,1,0:T(8,128)(2,1)} %get-tuple-element.205, s32[1024]{0:T(1024)S(1)} %pad_clamp_fusion.2), kind=kCustom, calls=%fused_computation.clone.clone.1 | custom fusion | bytes 9437472 | tf_op jit(solution)/shard_map/while/body/eval_jaxpr/gather | solution.py:57
  321.2 7.7 %reshape.197 = bf16[4,18,128,2,128]{4,3,2,1,0:T(2,128)(2,1)} reshape(bf16[72,128,256]{2,1,0:T(8,128)(2,1)} %gather_fusion.1) | data formatting | bytes 9437184 | tf_op jit(solution)/shard_map/while/body/eval_jaxpr/reshape | solution.py:57
  328.9 9.4 %fusion.52 = bf16[1,4,128,2,128]{2,4,3,1,0:T(8,128)(2,1)S(1)} fusion(f32[4,2,128,18,128]{2,4,3,1,0:T(8,128)} %bitcast.66, f32[4,2,128]{2,1,0:T(2,128)S(1)} %fusion.51, f32[4,2,128]{2,1,0:T(2,128)S(1)} %fusion.50, pred[4,128,18,128]{1,3,2,0:T(8,128)(4,1)S(1)} %compare_and_fusion.2, bf16[4,18,128,2,128]{4,3,2,1,0:T(2,128)(2,1)} %reshape.197), kind=kOutput, calls=%fused_computation.14.clone.1 | convolution fusion | flops 618266624 | bytes 15605760 | tf_op jit(solution)/shard_map/while/body/eval_jaxpr/bhqnk,bnkhd->bqhd/dot_general | solution.py:77
  339.0 3.5 compare_and_fusion.2
  342.6 8.8 %gather_fusion = bf16[72,128,256]{2,1,0:T(8,128)(2,1)} fusion(bf16[128,128,256]{2,1,0:T(8,128)(2,1)} %get-tuple-element.209, s32[1024]{0:T(1024)S(1)} %pad_clamp_fusion.2), kind=kCustom, calls=%fused_computation.1.clone.clone.1 | custom fusion | bytes 9437472 | tf_op jit(solution)/shard_map/while/body/eval_jaxpr/gather | solution.py:54
  351.4 7.7 %reshape.196 = bf16[4,18,128,2,128]{4,3,2,1,0:T(2,128)(2,1)} reshape(bf16[72,128,256]{2,1,0:T(8,128)(2,1)} %gather_fusion) | data formatting | bytes 9437184 | tf_op jit(solution)/shard_map/while/body/eval_jaxpr/reshape | solution.py:54
  359.2 3.6 copy.44
  370.5 8.8 %gather_fusion.1 = bf16[72,128,256]{2,1,0:T(8,128)(2,1)} fusion(bf16[128,128,256]{2,1,0:T(8,128)(2,1)} %get-tuple-element.205, s32[1024]{0:T(1024)S(1)} %pad_clamp_fusion.2), kind=kCustom, calls=%fused_computation.clone.clone.1 | custom fusion | bytes 9437472 | tf_op jit(solution)/shard_map/while/body/eval_jaxpr/gather | solution.py:57
  379.3 7.7 %reshape.197 = bf16[4,18,128,2,128]{4,3,2,1,0:T(2,128)(2,1)} reshape(bf16[72,128,256]{2,1,0:T(8,128)(2,1)} %gather_fusion.1) | data formatting | bytes 9437184 | tf_op jit(solution)/shard_map/while/body/eval_jaxpr/reshape | solution.py:57
  387.1 9.4 %fusion.52 = bf16[1,4,128,2,128]{2,4,3,1,0:T(8,128)(2,1)S(1)} fusion(f32[4,2,128,18,128]{2,4,3,1,0:T(8,128)} %bitcast.66, f32[4,2,128]{2,1,0:T(2,128)S(1)} %fusion.51, f32[4,2,128]{2,1,0:T(2,128)S(1)} %fusion.50, pred[4,128,18,128]{1,3,2,0:T(8,128)(4,1)S(1)} %compare_and_fusion.2, bf16[4,18,128,2,128]{4,3,2,1,0:T(2,128)(2,1)} %reshape.197), kind=kOutput, calls=%fused_computation.14.clone.1 | convolution fusion | flops 618266624 | bytes 15605760 | tf_op jit(solution)/shard_map/while/body/eval_jaxpr/bhqnk,bnkhd->bqhd/dot_general | solution.py:77
  397.1 7.2 %convolution_convert_fusion = bf16[1024,4096]{1,0:T(8,128)(2,1)} fusion(bf16[256,4096]{1,0:T(8,128)(2,1)} %all-gather.12.cloned.1.call-done, bf16[128,8,2,128]{3,2,1,0:T(2,128)(2,1)S(1)} %bitcast.70), kind=kOutput, calls=%fused_computation.33 | convolution fusion | flops 2151677952 | bytes 11010048 | tf_op jit(solution)/shard_map/dot_general | solution.py:92
  404.3 52.1 %reduce-scatter.2.cloned.1.call-done = bf16[128,4096]{1,0:T(8,128)(2,1)} async-done(((bf16[1024,4096]{1,0:T(8,128)(2,1)}), bf16[128,4096]{1,0:T(8,128)(2,1)}) %reduce-scatter.2.cloned.1.call-update) | async-done | bytes 1048592 | tf_op jit(solution)/shard_map/reduce_scatter | solution.py:91
  (58 shorter events, 19.5 us)
Async XLA Ops:
  6.5 132.4 %copy-start = (s32[128,16]{0,1:T(8,128)S(1)}, s32[128,16]{0,1:T(8,128)}, u32[]{:S(2)}) copy-start(s32[128,16]{0,1:T(8,128)} %param.11) | copy-start | bytes 24580
  6.5 67.2 %all-gather.10.cloned.1.call-start = ((), (), s32[]{:S(2)}) async-start(), calls=%async_computation.2 | async-start | bytes 6684672 | tf_op jit(solution)/shard_map/all_gather | solution.py:28
  7.3 118.4 %all-gather.8.cloned.1.call-start = ((), (), s32[]{:S(2)}) async-start(), calls=%async_computation.1 | async-start | bytes 9437184 | tf_op jit(solution)/shard_map/all_gather | solution.py:21
  11.4 196.5 %all-gather.14.cloned.1.call-start = ((), (), s32[]{:S(2)}) async-start(), calls=%async_computation.5 | async-start | bytes 8912896 | tf_op jit(solution)/shard_map/all_gather | solution.py:41
  137.7 142.7 %all-gather.16.cloned.1.call-start = ((), (), s32[]{:S(2)}) async-start(), calls=%async_computation.6 | async-start | bytes 8912896 | tf_op jit(solution)/shard_map/all_gather | solution.py:40
  138.2 258.9 %all-gather.12.cloned.1.call-start = ((), (), s32[]{:S(2)}) async-start(), calls=%async_computation.3 | async-start | bytes 2228224 | tf_op jit(solution)/shard_map/all_gather | solution.py:90
  138.8 317.6 %reduce-scatter.2.cloned.1.call-start = ((), (), s32[]{:S(2)}) async-start(), calls=%async_computation.4 | async-start | bytes 9437184 | tf_op jit(solution)/shard_map/reduce_scatter | solution.py:91
  306.0 3.6 copy-start.2
  364.3 3.7 copy-start.2
  397.1 59.3 %copy-start.1 = (s32[128,16]{0,1:T(8,128)S(1)}, s32[128,16]{0,1:T(8,128)}, u32[]{:S(2)}) copy-start(s32[128,16]{0,1:T(8,128)} %param.11) | copy-start | bytes 24580
Sparse Core Ops, SparseCore 0:
  9.5 64.1 all-gather.9
  75.4 50.1 all-gather.7
  137.8 70.0 all-gather.13
  209.9 70.3 all-gather.15
  282.3 45.1 all-gather.11
  404.4 51.9 reduce-scatter.1
where the time goes:
time: 464 us; the launch traced here: 463 us
  waiting for transfers between devices  309 us (67%)
  local copies, waits for them, and re-layouts  80.4 us (17%)
  matrix products  39.6 us (9%)
  other arithmetic  19.8 us (4%)
  between operations  13.5 us (3%)
    all_gather x1, waiting for transfers between devices, shards(): lax.all_gather(key_rows, 'ctx', axis=0, tiled=True)  72.4 us
    all_gather x1, waiting for transfers between devices, shards(): lax.all_gather(value_rows, 'ctx', axis=0, tiled=True)  68.6 us
    all_gather x1, waiting for transfers between devices, shards(): lax.all_gather(qkv_weight, 'ctx', axis=1, tiled=True)  62.3 us
    reduce_scatter x1, waiting for transfers between devices, shards(): lax.psum_scatter(jnp.dot(attended, projection, preferred_element_type=jnp...  52.1 us
    all_gather x1, waiting for transfers between devices, shards(): gathered = lax.all_gather(normed, 'fsdp', axis=0, tiled=True)  51.9 us
    reshape x4, local copies, waits for them, and re-layouts, attend(): pool_keys[group_index]  22.6 us
    dot_general x2, matrix products, attend(): jnp.einsum('bhqnk,bnkhd->bqhd', weights, value_blocks, preferred_element_...  18.8 us
    gather x2, local copies, waits for them, and re-layouts, attend(): pool_values[group_index]  17.8 us
  transfers between devices with their start and end apart: 6, of which 5 were waited for; matrix products, arithmetic and copies ran while one was open for 25% of the time, Pallas kernels for 0%

commit v1 on v0

--- a/solution.py
+++ b/solution.py
@@ -8,6 +8,28 @@
 BLK = 128
 SUMMARY = 16
 EPSILON = 1e-05
+
+
+def laid_out(tiles, dim):
+    shape = list(tiles.shape[1:])
+    shape[dim] *= tiles.shape[0]
+    return jnp.moveaxis(tiles, 0, dim).reshape(shape)
+
+
+def gather_around(x, axis, dim):
+    length = lax.axis_size(axis)
+    pairs = [(i, (i + 1) % length) for i in range(length)]
+    back = [(b, a) for a, b in pairs]
+    lower, upper = ([], [])
+    for step in range(length - 1):
+        if step % 2 == 0:
+            lower.append(lax.ppermute(lower[-1] if lower else x, axis, pairs))
+        else:
+            upper.append(lax.ppermute(upper[-1] if upper else x, axis, back))
+    parts = jnp.stack([*lower[::-1], x, *upper])
+    shift = lax.axis_index(axis) - len(lower)
+    parts = parts[(jnp.arange(length) - shift) % length]
+    return laid_out(parts, dim)
 
 
 def normalize(tokens, norm_gain):
@@ -38,7 +60,7 @@
     key_index = jnp.concatenate([own_blocks[:, None], own_blocks[:, None] - 1, listed], axis=1)
     every_key, every_value = (
         lax.all_gather(key_rows, "ctx", axis=0, tiled=True),
-        lax.all_gather(value_rows, "ctx", axis=0, tiled=True),
+        gather_around(value_rows, "ctx", 0),
     )
     total_blocks = every_key.shape[0] // BLK
     pool_keys = every_key.reshape(total_blocks, BLK, local_width)

time: 464 us -> 588 us (1.27)
  waiting for transfers between devices: 309 us -> 380 us
  starting transfers between devices: 0.2 us -> 31.2 us
  local copies, waits for them, and re-layouts: 80.4 us -> 100 us
    ppermute x0 -> x15, waiting for transfers between devices: none -> 198 us  [the longest x8 108 us: gather_around(): lower.append(lax.ppermute(lower[-1] if lower else x, axis, pairs))]
    all_gather x1, waiting for transfers between devices: 72.4 us -> 0.01 us  [shards(): lax.all_gather(key_rows, 'ctx', axis=0, tiled=True)]
    all_gather x1 -> x0, waiting for transfers between devices: 68.6 us -> none  [shards(): lax.all_gather(value_rows, 'ctx', axis=0, tiled=True)]
    ppermute x0 -> x15, starting transfers between devices: none -> 31.1 us  [the longest x7 29.8 us: gather_around(): upper.append(lax.ppermute(upper[-1] if upper else x, axis, back))]
    reduce_scatter x1, waiting for transfers between devices: 52.1 us -> 67.8 us  [shards(): lax.psum_scatter(jnp.dot(attended, projection, preferred_element_type=jnp...]
    unnamed x5 -> x21, local copies, waits for them, and re-layouts: 0.08 us -> 13.9 us
    gather x0 -> x1, local copies, waits for them, and re-layouts: none -> 8.42 us  [gather_around(): parts = parts[(jnp.arange(length) - shift) % length]]
  transfers between devices with their start and end apart: 6 -> 20, of which waited for: 5 -> 18; matrix products, arithmetic and copies ran while one was open for 25% -> 23% of each run, Pallas kernels for 0% -> 0%
where the time goes in v1:
time: 588 us; the launch traced here: 586 us
  waiting for transfers between devices  380 us (65%)
  local copies, waits for them, and re-layouts  100 us (17%)
  matrix products  39.7 us (7%)
  starting transfers between devices  31.2 us (5%)
  other arithmetic  21.1 us (4%)
  between operations  13.2 us (2%)
    ppermute x8, waiting for transfers between devices, gather_around(): lower.append(lax.ppermute(lower[-1] if lower else x, axis, pairs))  108 us
    ppermute x7, waiting for transfers between devices, gather_around(): upper.append(lax.ppermute(upper[-1] if upper else x, axis, back))  89.6 us
    reduce_scatter x1, waiting for transfers between devices, shards(): lax.psum_scatter(jnp.dot(attended, projection, preferred_element_type=jnp...  67.8 us
    all_gather x1, waiting for transfers between devices, shards(): lax.all_gather(qkv_weight, 'ctx', axis=1, tiled=True)  62.3 us
    all_gather x1, waiting for transfers between devices, shards(): gathered = lax.all_gather(normed, 'fsdp', axis=0, tiled=True)  51.9 us
    ppermute x7, starting transfers between devices, gather_around(): upper.append(lax.ppermute(upper[-1] if upper else x, axis, back))  29.8 us
    reshape x4, local copies, waits for them, and re-layouts, attend(): pool_keys[group_index]  22.6 us
    dot_general x2, matrix products, attend(): jnp.einsum('bhqnk,bnkhd->bqhd', weights, value_blocks, preferred_element_...  18.8 us
  transfers between devices with their start and end apart: 20, of which 18 were waited for; matrix products, arithmetic and copies ran while one was open for 23% of the time, Pallas kernels for 0%

profile of v1, /device:TPU:1, one launch (start us, length us, event | category | flops | bytes accessed | tf_op | source)
XLA Modules:
  0.0 586.4 jit_solution(16924199974314543804)
XLA Ops:
  11.4 62.3 %all-gather.8.cloned.1.call-done = bf16[3,4096,256]{2,1,0:T(8,128)(2,1)} async-done(((bf16[3,256,256]{2,1,0:T(8,128)(2,1)}), bf16[3,4096,256]{2,1,0:T(8,128)(2,1)}) %all-gather.8.cloned.1.call-update) | async-done | bytes 6291472 | tf_op jit(solution)/shard_map/all_gather | solution.py:50
  73.7 51.9 %all-gather.6.cloned.1.call-done = bf16[1024,4096]{1,0:T(8,128)(2,1)} async-done(((bf16[128,4096]{1,0:T(8,128)(2,1)}), bf16[1024,4096]{1,0:T(8,128)(2,1)}) %all-gather.6.cloned.1.call-update) | async-done | bytes 8388624 | tf_op jit(solution)/shard_map/all_gather | solution.py:43
  125.6 10.9 %fusion.30 = bf16[3,1024,256]{2,1,0:T(8,128)(2,1)S(1)} fusion(bf16[3,4096,256]{2,1,0:T(8,128)(2,1)} %all-gather.8.cloned.1.call-done, bf16[1024,4096]{1,0:T(8,128)(2,1)} %all-gather.6.cloned.1.call-done), kind=kOutput, calls=%fused_computation.41 | convolution fusion | flops 6443237376 | bytes 16252928 | tf_op jit(solution)/shard_map/td,cdi->cti/dot_general | solution.py:47
  137.9 15.3 %collective-permute-done = bf16[1024,256]{1,0:T(8,128)(2,1)S(1)} collective-permute-done((bf16[1024,256]{1,0:T(8,128)(2,1)S(1)}, bf16[1024,256]{1,0:T(8,128)(2,1)S(1)}, u32[]{:S(2)}, u32[]{:S(2)}) %collective-permute-start) | collective-permute-done | bytes 524320 | tf_op jit(solution)/shard_map/ppermute | solution.py:26
  153.2 15.7 %collective-permute-done.1 = bf16[1024,256]{1,0:T(8,128)(2,1)S(1)} collective-permute-done((bf16[1024,256]{1,0:T(8,128)(2,1)S(1)}, bf16[1024,256]{1,0:T(8,128)(2,1)S(1)}, u32[]{:S(2)}, u32[]{:S(2)}) %collective-permute-start.1) | collective-permute-done | bytes 524320 | tf_op jit(solution)/shard_map/ppermute | solution.py:26
  168.9 14.8 %collective-permute-done.2 = bf16[1024,256]{1,0:T(8,128)(2,1)S(1)} collective-permute-done((bf16[1024,256]{1,0:T(8,128)(2,1)S(1)}, bf16[1024,256]{1,0:T(8,128)(2,1)S(1)}, u32[]{:S(2)}, u32[]{:S(2)}) %collective-permute-start.2) | collective-permute-done | bytes 524320 | tf_op jit(solution)/shard_map/ppermute | solution.py:26
  183.7 14.0 %collective-permute-done.3 = bf16[1024,256]{1,0:T(8,128)(2,1)S(1)} collective-permute-done((bf16[1024,256]{1,0:T(8,128)(2,1)S(1)}, bf16[1024,256]{1,0:T(8,128)(2,1)S(1)}, u32[]{:S(2)}, u32[]{:S(2)}) %collective-permute-start.3) | collective-permute-done | bytes 524320 | tf_op jit(solution)/shard_map/ppermute | solution.py:26
  197.7 13.1 %collective-permute-done.4 = bf16[1024,256]{1,0:T(8,128)(2,1)S(1)} collective-permute-done((bf16[1024,256]{1,0:T(8,128)(2,1)S(1)}, bf16[1024,256]{1,0:T(8,128)(2,1)S(1)}, u32[]{:S(2)}, u32[]{:S(2)}) %collective-permute-start.4) | collective-permute-done | bytes 524320 | tf_op jit(solution)/shard_map/ppermute | solution.py:26
  210.8 12.3 %collective-permute-done.5 = bf16[1024,256]{1,0:T(8,128)(2,1)S(1)} collective-permute-done((bf16[1024,256]{1,0:T(8,128)(2,1)S(1)}, bf16[1024,256]{1,0:T(8,128)(2,1)S(1)}, u32[]{:S(2)}, u32[]{:S(2)}) %collective-permute-start.5) | collective-permute-done | bytes 524320 | tf_op jit(solution)/shard_map/ppermute | solution.py:26
  223.1 11.3 %collective-permute-done.6 = bf16[1024,256]{1,0:T(8,128)(2,1)S(1)} collective-permute-done((bf16[1024,256]{1,0:T(8,128)(2,1)S(1)}, bf16[1024,256]{1,0:T(8,128)(2,1)S(1)}, u32[]{:S(2)}, u32[]{:S(2)}) %collective-permute-start.6) | collective-permute-done | bytes 524320 | tf_op jit(solution)/shard_map/ppermute | solution.py:26
  234.5 11.5 %collective-permute-done.7 = bf16[1024,256]{1,0:T(8,128)(2,1)S(1)} collective-permute-done((bf16[1024,256]{1,0:T(8,128)(2,1)S(1)}, bf16[1024,256]{1,0:T(8,128)(2,1)S(1)}, u32[]{:S(2)}, u32[]{:S(2)}) %collective-permute-start.7) | collective-permute-done | bytes 524320 | tf_op jit(solution)/shard_map/ppermute | solution.py:26
  265.2 16.9 %collective-permute-done.9 = bf16[1024,256]{1,0:T(8,128)(2,1)S(1)} collective-permute-done((bf16[1024,256]{1,0:T(8,128)(2,1)S(1)}, bf16[1024,256]{1,0:T(8,128)(2,1)S(1)}, u32[]{:S(2)}, u32[]{:S(2)}) %collective-permute-start.9) | collective-permute-done | bytes 524320 | tf_op jit(solution)/shard_map/ppermute | solution.py:28
  299.8 17.8 %collective-permute-done.11 = bf16[1024,256]{1,0:T(8,128)(2,1)S(1)} collective-permute-done((bf16[1024,256]{1,0:T(8,128)(2,1)S(1)}, bf16[1024,256]{1,0:T(8,128)(2,1)S(1)}, u32[]{:S(2)}, u32[]{:S(2)}) %collective-permute-start.11) | collective-permute-done | bytes 524320 | tf_op jit(solution)/shard_map/ppermute | solution.py:28
  323.4 20.4 %collective-permute-done.12 = bf16[1024,256]{1,0:T(8,128)(2,1)} collective-permute-done((bf16[1024,256]{1,0:T(8,128)(2,1)S(1)}, bf16[1024,256]{1,0:T(8,128)(2,1)}, u32[]{:S(2)}, u32[]{:S(2)}) %collective-permute-start.12) | collective-permute-done | bytes 524320 | tf_op jit(solution)/shard_map/ppermute | solution.py:28
  350.8 14.0 %collective-permute-done.13 = bf16[1024,256]{1,0:T(8,128)(2,1)} collective-permute-done((bf16[1024,256]{1,0:T(8,128)(2,1)}, bf16[1024,256]{1,0:T(8,128)(2,1)}, u32[]{:S(2)}, u32[]{:S(2)}) %collective-permute-start.13) | collective-permute-done | bytes 524320 | tf_op jit(solution)/shard_map/ppermute | solution.py:28
  383.9 8.4 %gather_fusion.2 = bf16[16,1024,256]{2,1,0:T(8,128)(2,1)} fusion(bf16[16,1024,256]{2,1,0:T(8,128)(2,1)} %bitcast_dynamic-update-slice_fusion, s32[1024]{0:T(1024)} %pad_clamp_fusion.1), kind=kCustom, calls=%fused_computation.2 | custom fusion | bytes 16777280 | tf_op jit(solution)/shard_map/gather | solution.py:31
  392.3 112.4 %while.12 = (s32[]{:T(128)}, bf16[2,4,128,2,128]{4,3,2,1,0:T(2,128)(2,1)S(1)}, s32[2,4,18]{2,1,0:T(4,128)S(1)}, bf16[128,128,256]{2,1,0:T(8,128)(2,1)}, s32[2,4,...) while((s32[]{:T(128)}, ...), condition=%wide.region_4.5_spmd.clone.clone, body=%wide.region_1.4_spmd.clone.clone.sunk | while | flops 1243507456 | bytes 139060496 | solution.py:110
  396.2 8.9 %gather_fusion = bf16[72,128,256]{2,1,0:T(8,128)(2,1)} fusion(bf16[128,128,256]{2,1,0:T(8,128)(2,1)} %get-tuple-element.209, s32[1024]{0:T(1024)S(1)} %pad_clamp_fusion.3), kind=kCustom, calls=%fused_computation.1.clone.clone.1 | custom fusion | bytes 9437472 | tf_op jit(solution)/shard_map/while/body/eval_jaxpr/gather | solution.py:76
  422.1 8.9 %gather_fusion.1 = bf16[72,128,256]{2,1,0:T(8,128)(2,1)} fusion(bf16[128,128,256]{2,1,0:T(8,128)(2,1)} %get-tuple-element.205, s32[1024]{0:T(1024)S(1)} %pad_clamp_fusion.3), kind=kCustom, calls=%fused_computation.clone.clone.1 | custom fusion | bytes 9437472 | tf_op jit(solution)/shard_map/while/body/eval_jaxpr/gather | solution.py:79
  438.7 9.4 %fusion.54 = bf16[1,4,128,2,128]{2,4,3,1,0:T(8,128)(2,1)S(1)} fusion(f32[4,2,128,18,128]{2,4,3,1,0:T(8,128)} %bitcast.100, f32[4,2,128]{2,1,0:T(2,128)S(1)} %fusion.53, f32[4,2,128]{2,1,0:T(2,128)S(1)} %fusion.52, pred[4,128,18,128]{1,3,2,0:T(8,128)(4,1)S(1)} %compare_and_fusion.2, bf16[4,18,128,2,128]{4,3,2,1,0:T(2,128)(2,1)} %reshape.248), kind=kOutput, calls=%fused_computation.15.clone.1 | convolution fusion | flops 618266624 | bytes 15605760 | tf_op jit(solution)/shard_map/while/body/eval_jaxpr/bhqnk,bnkhd->bqhd/dot_general | solution.py:99
  452.4 8.9 %gather_fusion = bf16[72,128,256]{2,1,0:T(8,128)(2,1)} fusion(bf16[128,128,256]{2,1,0:T(8,128)(2,1)} %get-tuple-element.209, s32[1024]{0:T(1024)S(1)} %pad_clamp_fusion.3), kind=kCustom, calls=%fused_computation.1.clone.clone.1 | custom fusion | bytes 9437472 | tf_op jit(solution)/shard_map/while/body/eval_jaxpr/gather | solution.py:76
  478.2 8.8 %gather_fusion.1 = bf16[72,128,256]{2,1,0:T(8,128)(2,1)} fusion(bf16[128,128,256]{2,1,0:T(8,128)(2,1)} %get-tuple-element.205, s32[1024]{0:T(1024)S(1)} %pad_clamp_fusion.3), kind=kCustom, calls=%fused_computation.clone.clone.1 | custom fusion | bytes 9437472 | tf_op jit(solution)/shard_map/while/body/eval_jaxpr/gather | solution.py:79
  494.8 9.4 %fusion.54 = bf16[1,4,128,2,128]{2,4,3,1,0:T(8,128)(2,1)S(1)} fusion(f32[4,2,128,18,128]{2,4,3,1,0:T(8,128)} %bitcast.100, f32[4,2,128]{2,1,0:T(2,128)S(1)} %fusion.53, f32[4,2,128]{2,1,0:T(2,128)S(1)} %fusion.52, pred[4,128,18,128]{1,3,2,0:T(8,128)(4,1)S(1)} %compare_and_fusion.2, bf16[4,18,128,2,128]{4,3,2,1,0:T(2,128)(2,1)} %reshape.248), kind=kOutput, calls=%fused_computation.15.clone.1 | convolution fusion | flops 618266624 | bytes 15605760 | tf_op jit(solution)/shard_map/while/body/eval_jaxpr/bhqnk,bnkhd->bqhd/dot_general | solution.py:99
  512.1 67.8 %reduce-scatter.2.cloned.1.call-done = bf16[128,4096]{1,0:T(8,128)(2,1)} async-done(((bf16[1024,4096]{1,0:T(8,128)(2,1)}), bf16[128,4096]{1,0:T(8,128)(2,1)}) %reduce-scatter.2.cloned.1.call-update) | async-done | bytes 1048592 | tf_op jit(solution)/shard_map/reduce_scatter | solution.py:113
  (106 shorter events, 140.0 us)
Async XLA Ops:
  6.5 316.7 %copy-start = (s32[128,16]{0,1:T(8,128)S(1)}, s32[128,16]{0,1:T(8,128)}, u32[]{:S(2)}) copy-start(s32[128,16]{0,1:T(8,128)} %param.11) | copy-start | bytes 24580
  6.5 67.2 %all-gather.8.cloned.1.call-start = ((), (), s32[]{:S(2)}) async-start(), calls=%async_computation.2 | async-start | bytes 6684672 | tf_op jit(solution)/shard_map/all_gather | solution.py:50
  7.3 118.4 %all-gather.6.cloned.1.call-start = ((), (), s32[]{:S(2)}) async-start(), calls=%async_computation.1 | async-start | bytes 9437184 | tf_op jit(solution)/shard_map/all_gather | solution.py:43
  11.4 380.9 %all-gather.12.cloned.1.call-start = ((), (), s32[]{:S(2)}) async-start(), calls=%async_computation.5 | async-start | bytes 8912896 | tf_op jit(solution)/shard_map/all_gather | solution.py:62
  136.6 16.6 %collective-permute-start = (bf16[1024,256]{1,0:T(8,128)(2,1)S(1)}, bf16[1024,256]{1,0:T(8,128)(2,1)S(1)}, u32[]{:S(2)}, u32[]{:S(2)}) collective-permute-start(bf16[1024,256]{1,0:T(8,128)(2,1)S(1)} %slice_bitcast_fusion), channel_id=1, source_target_pairs={{0,8},{8,16},{16,24},{24,32},{32,40},{40,48},{48,56},{56,64},{64,7... | collective-permute-start | bytes 1572872 | tf_op jit(solution)/shard_map/ppermute | solution.py:26
  153.2 15.7 %collective-permute-start.1 = (bf16[1024,256]{1,0:T(8,128)(2,1)S(1)}, bf16[1024,256]{1,0:T(8,128)(2,1)S(1)}, u32[]{:S(2)}, u32[]{:S(2)}) collective-permute-start(bf16[1024,256]{1,0:T(8,128)(2,1)S(1)} %collective-permute-done), channel_id=1, source_target_pairs={{0,8},{8,16},{16,24},{24,32},{32,40},{40,48},{48,56},{56,64},{64,7... | collective-permute-start | bytes 1572872 | tf_op jit(solution)/shard_map/ppermute | solution.py:26
  168.9 14.8 %collective-permute-start.2 = (bf16[1024,256]{1,0:T(8,128)(2,1)S(1)}, bf16[1024,256]{1,0:T(8,128)(2,1)S(1)}, u32[]{:S(2)}, u32[]{:S(2)}) collective-permute-start(bf16[1024,256]{1,0:T(8,128)(2,1)S(1)} %collective-permute-done.1), channel_id=1, source_target_pairs={{0,8},{8,16},{16,24},{24,32},{32,40},{40,48},{48,56},{56,64},{64,7... | collective-permute-start | bytes 1572872 | tf_op jit(solution)/shard_map/ppermute | solution.py:26
  183.7 14.0 %collective-permute-start.3 = (bf16[1024,256]{1,0:T(8,128)(2,1)S(1)}, bf16[1024,256]{1,0:T(8,128)(2,1)S(1)}, u32[]{:S(2)}, u32[]{:S(2)}) collective-permute-start(bf16[1024,256]{1,0:T(8,128)(2,1)S(1)} %collective-permute-done.2), channel_id=1, source_target_pairs={{0,8},{8,16},{16,24},{24,32},{32,40},{40,48},{48,56},{56,64},{64,7... | collective-permute-start | bytes 1572872 | tf_op jit(solution)/shard_map/ppermute | solution.py:26
  197.7 13.1 %collective-permute-start.4 = (bf16[1024,256]{1,0:T(8,128)(2,1)S(1)}, bf16[1024,256]{1,0:T(8,128)(2,1)S(1)}, u32[]{:S(2)}, u32[]{:S(2)}) collective-permute-start(bf16[1024,256]{1,0:T(8,128)(2,1)S(1)} %collective-permute-done.3), channel_id=1, source_target_pairs={{0,8},{8,16},{16,24},{24,32},{32,40},{40,48},{48,56},{56,64},{64,7... | collective-permute-start | bytes 1572872 | tf_op jit(solution)/shard_map/ppermute | solution.py:26
  210.8 12.3 %collective-permute-start.5 = (bf16[1024,256]{1,0:T(8,128)(2,1)S(1)}, bf16[1024,256]{1,0:T(8,128)(2,1)S(1)}, u32[]{:S(2)}, u32[]{:S(2)}) collective-permute-start(bf16[1024,256]{1,0:T(8,128)(2,1)S(1)} %collective-permute-done.4), channel_id=1, source_target_pairs={{0,8},{8,16},{16,24},{24,32},{32,40},{40,48},{48,56},{56,64},{64,7... | collective-permute-start | bytes 1572872 | tf_op jit(solution)/shard_map/ppermute | solution.py:26
  223.1 11.4 %collective-permute-start.6 = (bf16[1024,256]{1,0:T(8,128)(2,1)S(1)}, bf16[1024,256]{1,0:T(8,128)(2,1)S(1)}, u32[]{:S(2)}, u32[]{:S(2)}) collective-permute-start(bf16[1024,256]{1,0:T(8,128)(2,1)S(1)} %collective-permute-done.5), channel_id=1, source_target_pairs={{0,8},{8,16},{16,24},{24,32},{32,40},{40,48},{48,56},{56,64},{64,7... | collective-permute-start | bytes 1572872 | tf_op jit(solution)/shard_map/ppermute | solution.py:26
  234.5 11.5 %collective-permute-start.7 = (bf16[1024,256]{1,0:T(8,128)(2,1)S(1)}, bf16[1024,256]{1,0:T(8,128)(2,1)S(1)}, u32[]{:S(2)}, u32[]{:S(2)}) collective-permute-start(bf16[1024,256]{1,0:T(8,128)(2,1)S(1)} %collective-permute-done.6), channel_id=1, source_target_pairs={{0,8},{8,16},{16,24},{24,32},{32,40},{40,48},{48,56},{56,64},{64,7... | collective-permute-start | bytes 1572872 | tf_op jit(solution)/shard_map/ppermute | solution.py:26
  253.7 251.1 %all-gather.10.cloned.1.call-start = ((), (), s32[]{:S(2)}) async-start(), calls=%async_computation.3 | async-start | bytes 2228224 | tf_op jit(solution)/shard_map/all_gather | solution.py:112
  253.8 8.1 %collective-permute-start.8 = (bf16[1024,256]{1,0:T(8,128)(2,1)S(1)}, bf16[1024,256]{1,0:T(8,128)(2,1)S(1)}, u32[]{:S(2)}, u32[]{:S(2)}) collective-permute-start(bf16[1024,256]{1,0:T(8,128)(2,1)S(1)} %slice_bitcast_fusion), channel_id=1, source_target_pairs={{8,0},{16,8},{24,16},{32,24},{40,32},{48,40},{56,48},{64,56},{72,6... | collective-permute-start | bytes 1572872 | tf_op jit(solution)/shard_map/ppermute | solution.py:28
  261.9 20.2 %collective-permute-start.9 = (bf16[1024,256]{1,0:T(8,128)(2,1)S(1)}, bf16[1024,256]{1,0:T(8,128)(2,1)S(1)}, u32[]{:S(2)}, u32[]{:S(2)}) collective-permute-start(bf16[1024,256]{1,0:T(8,128)(2,1)S(1)} %collective-permute-done.8), channel_id=1, source_target_pairs={{8,0},{16,8},{24,16},{32,24},{40,32},{48,40},{56,48},{64,56},{72,6... | collective-permute-start | bytes 1572872 | tf_op jit(solution)/shard_map/ppermute | solution.py:28
  282.0 12.8 %collective-permute-start.10 = (bf16[1024,256]{1,0:T(8,128)(2,1)S(1)}, bf16[1024,256]{1,0:T(8,128)(2,1)S(1)}, u32[]{:S(2)}, u32[]{:S(2)}) collective-permute-start(bf16[1024,256]{1,0:T(8,128)(2,1)S(1)} %collective-permute-done.9), channel_id=1, source_target_pairs={{8,0},{16,8},{24,16},{32,24},{40,32},{48,40},{56,48},{64,56},{72,6... | collective-permute-start | bytes 1572872 | tf_op jit(solution)/shard_map/ppermute | solution.py:28
  294.9 22.8 %collective-permute-start.11 = (bf16[1024,256]{1,0:T(8,128)(2,1)S(1)}, bf16[1024,256]{1,0:T(8,128)(2,1)S(1)}, u32[]{:S(2)}, u32[]{:S(2)}) collective-permute-start(bf16[1024,256]{1,0:T(8,128)(2,1)S(1)} %collective-permute-done.10), channel_id=1, source_target_pairs={{8,0},{16,8},{24,16},{32,24},{40,32},{48,40},{56,48},{64,56},{72,6... | collective-permute-start | bytes 1572872 | tf_op jit(solution)/shard_map/ppermute | solution.py:28
  317.6 26.2 %collective-permute-start.12 = (bf16[1024,256]{1,0:T(8,128)(2,1)S(1)}, bf16[1024,256]{1,0:T(8,128)(2,1)}, u32[]{:S(2)}, u32[]{:S(2)}) collective-permute-start(bf16[1024,256]{1,0:T(8,128)(2,1)S(1)} %collective-permute-done.11), channel_id=1, source_target_pairs={{8,0},{16,8},{24,16},{32,24},{40,32},{48,40},{56,48},{64,56},{72,6... | collective-permute-start | bytes 1572872 | tf_op jit(solution)/shard_map/ppermute | solution.py:28
  323.2 256.7 %reduce-scatter.2.cloned.1.call-start = ((), (), s32[]{:S(2)}) async-start(), calls=%async_computation.4 | async-start | bytes 9437184 | tf_op jit(solution)/shard_map/reduce_scatter | solution.py:113
  343.8 21.0 %collective-permute-start.13 = (bf16[1024,256]{1,0:T(8,128)(2,1)}, bf16[1024,256]{1,0:T(8,128)(2,1)}, u32[]{:S(2)}, u32[]{:S(2)}) collective-permute-start(bf16[1024,256]{1,0:T(8,128)(2,1)} %collective-permute-done.12), channel_id=1, source_target_pairs={{8,0},{16,8},{24,16},{32,24},{40,32},{48,40},{56,48},{64,56},{72,6... | collective-permute-start | bytes 1572872 | tf_op jit(solution)/shard_map/ppermute | solution.py:28
  364.8 17.1 %collective-permute-start.14 = (bf16[1024,256]{1,0:T(8,128)(2,1)}, bf16[1024,256]{1,0:T(8,128)(2,1)}, u32[]{:S(2)}, u32[]{:S(2)}) collective-permute-start(bf16[1024,256]{1,0:T(8,128)(2,1)} %collective-permute-done.13), channel_id=1, source_target_pairs={{8,0},{16,8},{24,16},{32,24},{40,32},{48,40},{56,48},{64,56},{72,6... | collective-permute-start | bytes 1572872 | tf_op jit(solution)/shard_map/ppermute | solution.py:28
  383.9 8.4 %copy-start.3 = (s32[2,4]{1,0:T(2,128)S(1)}, s32[2,4]{1,0:T(2,128)}, u32[]{:S(2)}) copy-start(s32[2,4]{1,0:T(2,128)} %add_add_fusion.1) | copy-start | bytes 100
  418.0 4.1 copy-start.2
  504.8 75.1 %copy-start.1 = (s32[128,16]{0,1:T(8,128)S(1)}, s32[128,16]{0,1:T(8,128)}, u32[]{:S(2)}) copy-start(s32[128,16]{0,1:T(8,128)} %param.11) | copy-start | bytes 24580
  (1 other events, 4.1 us)
Sparse Core Ops, SparseCore 0:
  9.5 64.1 all-gather.7
  75.4 50.1 all-gather.5
  253.8 109.1 all-gather.11
  365.0 49.2 all-gather.9
  512.2 67.6 reduce-scatter.1
